TPU v7x, 32 devices: a whole 2x2x4 slice. The times are simulated.
32 devices in a mesh: ctx: 8 (over z, y), pack: 4 (over x, core).
Axes of the slice: x: 2, y: 2, z: 4, core: 2. Of those that a mesh axis runs over, the one named last changes fastest.
Arguments:
- hidden: bfloat16 [8192, 2048], P(('ctx', 'pack')), may hold values from -4 to 4
- first_keys: bfloat16 [8192, 2048], P('ctx', 'pack'), may hold values from -400 to 400
- first_values: bfloat16 [8192, 2048], P('ctx', 'pack'), may hold values from -18 to 18
- w_query: bfloat16 [2048, 2048], P(None, 'pack'), may hold values from -0.125 to 0.125
- w_out: bfloat16 [2048, 2048], P('pack'), may hold values from -0.125 to 0.125
- norm_gain: float32 [2048], replicated, may hold values from 0.1 to 1.9
- router_weight: float32 [2048], replicated, may hold values from -0.5 to 0.5
- route_list: int32 [8, 256], P('ctx'), may hold values from 0 to 1023, as said below
- pack_order: int32 [8, 256], P('ctx'), may hold values from 0 to 255, each once within a row
- pattern: int32 [8, 12], replicated, may hold values from 0 to 7
Outputs:
- hidden_out: bfloat16 [8192, 2048], P(('ctx', 'pack'))
- packed_states: bfloat16 [2048, 2048], P(('ctx', 'pack'))
Inputs may be any that keep to these rules, and one draw needn't show every extreme that they name: `route_list`: each row lists 256 distinct span-local positions in ascending order. At most 96 of a row's positions lie among the 256 tokens of one device, and in every row some device holds exactly 96.
All inputs are finite; a program needn't handle non-finite values.
Results may differ from a plain program's by a relative error of at most 0.023.
Values may be sent and summed in bfloat16 or wider, within the bound.
No kernel may reach another device: no remote copies, remote signals or barrier semaphores. Data moves between devices by JAX's collectives and lax.ppermute only.
A program may use at most 128 MiB of HBM per device.

v0:
```python
import math
import jax
import jax.numpy as jnp
from jax import lax
from jax.sharding import PartitionSpec as P

HD = 128
epsilon = 1e-06
very_negative = -1e30


def rotate(projected, position, head_count):
    row_count = projected.shape[0]
    head_size = projected.shape[1] // head_count
    half_size = head_size // 2
    frequency = 10000.0 ** (-jnp.arange(half_size, dtype=jnp.float32) * 2.0 / head_size)
    angle = position.astype(jnp.float32)[:, None] * frequency[None, :]
    cosine = jnp.cos(angle)[:, None, :]
    sine_part = jnp.sin(angle)[:, None, :]
    shaped = projected.reshape(row_count, head_count, head_size)
    front_half = shaped[..., :half_size]
    back_half = shaped[..., half_size:]
    turned = jnp.concatenate(
        [front_half * cosine - back_half * sine_part, back_half * cosine + front_half * sine_part],
        axis=-1,
    )
    return turned.reshape(row_count, head_count * head_size)


def partial_block(query_heads, key_heads, value_heads, allowed):
    scale_factor = 1.0 / math.sqrt(query_heads.shape[2])
    scores = (
        jnp.einsum("qhd,khd->hqk", query_heads, key_heads, preferred_element_type=jnp.float32)
        * scale_factor
    )
    if allowed is not None:
        scores = jnp.where(allowed[None], scores, very_negative)
    row_peak = jnp.max(scores, axis=-1)
    weights = jnp.exp(scores - row_peak[..., None])
    if allowed is not None:
        weights = jnp.where(allowed[None], weights, 0.0)
    weight_sum = jnp.sum(weights, axis=-1)
    rounded = weights.astype(jnp.bfloat16)
    summed = jnp.einsum("hqk,khd->qhd", rounded, value_heads, preferred_element_type=jnp.float32)
    return (row_peak, weight_sum, summed)


def merge(former, latter):
    new_peak = jnp.maximum(former[0], latter[0])
    former_scale = jnp.exp(former[0] - new_peak)
    latter_scale = jnp.exp(latter[0] - new_peak)
    weight_sum = former_scale * former[1] + latter_scale * latter[1]
    summed = (
        jnp.transpose(former_scale)[:, :, None] * former[2]
        + jnp.transpose(latter_scale)[:, :, None] * latter[2]
    )
    return (new_peak, weight_sum, summed)


def local(
    hidden,
    first_keys,
    first_values,
    w_query,
    w_out,
    norm_gain,
    router_weight,
    route_list,
    pack_order,
    pattern,
):
    n_pack = lax.axis_size("pack")
    span_id = lax.axis_index("ctx")
    pack_id = lax.axis_index("pack")
    tok_dev = hidden.shape[0]
    model_width = hidden.shape[1]
    span_len = tok_dev * n_pack
    routes = route_list[0]
    slot_order = pack_order[0]
    routed = routes.shape[0]
    per_slot = routed // n_pack
    capacity = 3 * tok_dev // 8
    local_width = first_keys.shape[1]
    head_count = local_width // HD
    lane_ids = jnp.arange(n_pack, dtype=jnp.int32)
    starts = jnp.sum((routes[None, :] < (lane_ids * tok_dev)[:, None]).astype(jnp.int32), axis=1)
    run_ends = jnp.concatenate([starts[1:], jnp.full((1,), routed, jnp.int32)])
    my_start = jnp.sum(jnp.where(lane_ids == pack_id, starts, 0))
    my_count = jnp.sum(jnp.where(lane_ids == pack_id, run_ends - starts, 0))
    padded = jnp.concatenate([routes, jnp.full((capacity,), span_len, jnp.int32)])
    sending = lax.dynamic_slice_in_dim(padded, my_start, capacity, 0)
    is_valid = jnp.arange(capacity, dtype=jnp.int32) < my_count
    local_rows = jnp.clip(sending - pack_id * tok_dev, 0, tok_dev - 1)
    outgoing = jnp.where(is_valid[:, None], hidden[local_rows], jnp.zeros((), hidden.dtype))
    gathered = lax.all_gather(outgoing, "pack", axis=0, tiled=True)
    picked = routes[slot_order]
    owner_id = picked // tok_dev
    owner_start = jnp.sum(
        jnp.where(owner_id[:, None] == lane_ids[None, :], starts[None, :], 0), axis=1
    )
    source_row = owner_id * capacity + (slot_order - owner_start)
    routed_rows = gathered[source_row]
    position = span_id * span_len + picked
    rows_float = routed_rows.astype(jnp.float32)
    mean_square = jnp.mean(rows_float * rows_float, axis=-1, keepdims=True)
    normed = (rows_float * lax.rsqrt(mean_square + epsilon) * norm_gain).astype(jnp.bfloat16)
    queries = rotate(
        jnp.dot(normed, w_query, preferred_element_type=jnp.float32), position, head_count
    ).astype(jnp.bfloat16)
    query_heads = queries.reshape(routed, head_count, HD)
    key_heads = first_keys.reshape(span_len, head_count, HD)
    value_heads = first_values.reshape(span_len, head_count, HD)
    key_pos = span_id * span_len + jnp.arange(span_len, dtype=jnp.int32)
    own_state = partial_block(
        query_heads, key_heads, value_heads, key_pos[None, :] <= position[:, None]
    )
    wanted = pattern[span_id]
    running = own_state
    key_piece = lax.all_gather(first_keys, "ctx", axis=0, tiled=True)
    value_piece = lax.all_gather(first_values, "ctx", axis=0, tiled=True)
    blocks = key_piece.shape[0] // span_len
    key_stack = key_piece.reshape(blocks, span_len, head_count, HD)
    value_stack = value_piece.reshape(blocks, span_len, head_count, HD)

    def visit(held, block_item):
        block_idx, key_block, value_block = block_item
        active = jnp.logical_and(block_idx < span_id, jnp.any(wanted == block_idx))
        held = lax.cond(
            active,
            lambda inner: merge(inner, partial_block(query_heads, key_block, value_block, None)),
            lambda inner: inner,
            held,
        )
        return (held, None)

    running, unused = lax.scan(
        visit, running, (jnp.arange(blocks, dtype=jnp.int32), key_stack, value_stack)
    )
    attended = (
        (running[2] / jnp.transpose(running[1])[:, :, None])
        .reshape(routed, local_width)
        .astype(jnp.bfloat16)
    )
    mixed = lax.psum_scatter(
        jnp.dot(attended, w_out, preferred_element_type=jnp.float32),
        "pack",
        scatter_dimension=0,
        tiled=True,
    )
    own_rows = lax.dynamic_slice_in_dim(rows_float, pack_id * per_slot, per_slot, 0)
    gate_value = jax.nn.sigmoid(jnp.dot(own_rows, router_weight, precision=lax.Precision.HIGHEST))
    packed_states = (own_rows + gate_value[:, None] * mixed).astype(jnp.bfloat16)
    target = jnp.where(is_valid, sending - pack_id * tok_dev, tok_dev)
    slot_rows = lax.dynamic_slice_in_dim(source_row, pack_id * per_slot, per_slot, 0)
    returning = (
        jnp.zeros((n_pack * capacity, model_width), jnp.float32)
        .at[slot_rows]
        .set(packed_states.astype(jnp.float32))
    )
    arrived = lax.psum_scatter(
        returning.astype(jnp.bfloat16), "pack", scatter_dimension=0, tiled=True
    )
    hidden_out = hidden.at[target].set(arrived, mode="drop")
    return (hidden_out, packed_states)


def solution(mesh):
    return jax.shard_map(
        local,
        mesh=mesh,
        in_specs=(
            P(("ctx", "pack"), None),
            P("ctx", "pack"),
            P("ctx", "pack"),
            P(None, "pack"),
            P("pack", None),
            P(),
            P(),
            P("ctx", None),
            P("ctx", None),
            P(),
        ),
        out_specs=(P(("ctx", "pack"), None), P(("ctx", "pack"), None)),
        check_vma=False,
    )
```

profile of v0, /device:TPU:0, one launch (start us, length us, event | category | flops | bytes accessed | tf_op | source)
XLA Modules:
  0.0 461.3 jit_solution(13582422450582323742)
XLA Ops:
  7.2 1.4 copy.80
  13.4 2.0 compare_select_fusion.2
  16.3 1.5 broadcast_select_fusion
  19.4 1.9 gather_fusion
  23.7 16.7 %all-gather.4.cloned.1.call-done = bf16[384,2048]{1,0:T(8,128)(2,1)} async-done(((bf16[96,2048]{1,0:T(8,128)(2,1)}), bf16[384,2048]{1,0:T(8,128)(2,1)}) %all-gather.4.cloned.1.call-update) | async-done | bytes 1572880 | tf_op jit(solution)/shard_map/all_gather | solution.py:95
  40.3 4.9 %gather_fusion.2 = bf16[256,2048]{1,0:T(8,128)(2,1)} fusion(bf16[384,2048]{1,0:T(8,128)(2,1)} %all-gather.4.cloned.1.call-done, s32[1024]{0:T(1024)S(1)} %pad_clamp_fusion), kind=kCustom, calls=%fused_computation.2 | custom fusion | bytes 2098176 | tf_op jit(solution)/shard_map/gather | solution.py:102
  45.3 1.5 multiply_reduce_fusion
  46.8 3.5 fusion.41
  50.3 2.1 reshape.245
  52.4 1.6 fusion.62
  54.3 2.0 fusion.26
  56.4 1.5 fusion.28
  57.9 2.3 fusion.34
  60.2 106.8 %all-gather.6.cloned.1.call-done = bf16[8192,512]{1,0:T(8,128)(2,1)} async-done(((bf16[1024,512]{1,0:T(8,128)(2,1)}), bf16[8192,512]{1,0:T(8,128)(2,1)}) %all-gather.6.cloned.1.call-update) | async-done | bytes 8388624 | tf_op jit(solution)/shard_map/all_gather | solution.py:119
  167.0 12.7 %reshape.295 = bf16[8,1024,4,128]{3,2,1,0:T(4,128)(2,1)} reshape(bf16[8192,512]{1,0:T(8,128)(2,1)} %all-gather.6.cloned.1.call-done) | data formatting | bytes 16777216 | tf_op jit(solution)/shard_map/reshape | solution.py:122
  179.7 8.7 %copy.34 = bf16[8,1024,4,128]{3,1,2,0:T(8,128)(2,1)} copy(bf16[8,1024,4,128]{3,2,1,0:T(4,128)(2,1)} %reshape.295) | data formatting | bytes 16777216 | tf_op jit(solution)/shard_map/while | solution.py:136
  188.4 103.4 %all-gather.8.cloned.1.call-done = bf16[8192,512]{1,0:T(8,128)(2,1)} async-done(((bf16[1024,512]{1,0:T(8,128)(2,1)}), bf16[8192,512]{1,0:T(8,128)(2,1)}) %all-gather.8.cloned.1.call-update) | async-done | bytes 8388624 | tf_op jit(solution)/shard_map/all_gather | solution.py:120
  291.8 12.5 %reshape.296 = bf16[8,1024,4,128]{3,2,1,0:T(4,128)(2,1)} reshape(bf16[8192,512]{1,0:T(8,128)(2,1)} %all-gather.8.cloned.1.call-done) | data formatting | bytes 16777216 | tf_op jit(solution)/shard_map/reshape | solution.py:123
  304.3 8.7 %copy.35 = bf16[8,1024,4,128]{3,1,2,0:T(8,128)(2,1)} copy(bf16[8,1024,4,128]{3,2,1,0:T(4,128)(2,1)} %reshape.296) | data formatting | bytes 16777216 | tf_op jit(solution)/shard_map/while | solution.py:136
  313.0 25.6 %while.14 = (s32[]{:T(128)}, f32[4,256]{1,0:T(4,128)S(1)}, f32[4,256]{1,0:T(4,128)S(1)}, f32[256,4,128]{2,0,1:T(8,128)}, s32[8]{0:T(128)S(1)}, /*index=5*/s32[]{...) while((s32[]{:T(128)}, f32[4,256]{1,0:T(4,128)S(1)}, ...), condition=%wide.region_13.14_spmd, body=%wide.region_7.13_spmd.sunk | while | flops 545657856 | bytes 20264304 | solution.py:136
  314.3 1.3 compare_reduce_fusion.2
  323.9 1.3 compare_reduce_fusion.2
  333.5 1.3 compare_reduce_fusion.2
  338.6 2.0 copy.36
  341.7 2.1 fusion.63
  344.0 2.8 convert_element_type.45
  348.0 68.0 %reduce-scatter.3.cloned.1.call-done = f32[64,2048]{1,0:T(8,128)} async-done(((f32[256,2048]{1,0:T(8,128)}), f32[64,2048]{1,0:T(8,128)}) %reduce-scatter.3.cloned.1.call-update) | async-done | bytes 524304 | tf_op jit(solution)/shard_map/reduce_scatter | solution.py:144
  416.0 1.3 add_convert_fusion
  417.4 2.8 scatter_custom_fusion
  420.1 3.3 convert_element_type.53
  423.4 28.1 %reduce-scatter.5.cloned.1.call-done = bf16[96,2048]{1,0:T(8,128)(2,1)} async-done(((bf16[384,2048]{1,0:T(8,128)(2,1)}), bf16[96,2048]{1,0:T(8,128)(2,1)}) %reduce-scatter.5.cloned.1.call-update) | async-done | bytes 393232 | tf_op jit(solution)/shard_map/reduce_scatter | solution.py:160
  451.6 2.2 scatter_fusion
  (79 shorter events, 22.8 us)
Async XLA Ops:
  7.2 334.6 %copy-start = (bf16[512,2048]{1,0:T(8,128)(2,1)S(1)}, bf16[512,2048]{1,0:T(8,128)(2,1)}, u32[]{:S(2)}) copy-start(bf16[512,2048]{1,0:T(8,128)(2,1)} %param.18) | copy-start | bytes 6291460
  7.2 12.2 %copy-start.1 = (s32[1,256]{1,0:T(1,128)S(1)}, s32[1,256]{1,0:T(1,128)}, u32[]{:S(2)}) copy-start(s32[1,256]{1,0:T(1,128)} %param.21) | copy-start | bytes 3076
  7.2 12.2 %copy-start.9 = (s32[1,256]{1,0:T(1,128)S(1)}, s32[1,256]{1,0:T(1,128)}, u32[]{:S(2)}) copy-start(s32[1,256]{1,0:T(1,128)} %param.22) | copy-start | bytes 3076
  7.2 33.1 %all-gather.4.cloned.1.call-start = ((), (), s32[]{:S(2)}) async-start(), calls=%async_computation.2 | async-start | bytes 1966080 | tf_op jit(solution)/shard_map/all_gather | solution.py:95
  17.8 149.1 %all-gather.6.cloned.1.call-start = ((), (), s32[]{:S(2)}) async-start(), calls=%async_computation.3 | async-start | bytes 9437184 | tf_op jit(solution)/shard_map/all_gather | solution.py:119
  18.6 273.2 %all-gather.8.cloned.1.call-start = ((), (), s32[]{:S(2)}) async-start(), calls=%async_computation.4 | async-start | bytes 9437184 | tf_op jit(solution)/shard_map/all_gather | solution.py:120
  19.3 396.7 %reduce-scatter.3.cloned.1.call-start = ((), (), s32[]{:S(2)}) async-start(), calls=%async_computation.5 | async-start | bytes 2621440 | tf_op jit(solution)/shard_map/reduce_scatter | solution.py:144
  23.7 23.1 %copy-start.12 = (f32[2048]{0:T(1024)S(1)}, f32[2048]{0:T(1024)}, u32[]{:S(2)}) copy-start(f32[2048]{0:T(1024)} %param.19) | copy-start | bytes 24580
  52.4 2.0 copy-start.5
  54.0 2.4 copy-start.6
  54.3 3.6 copy-start.7
  341.7 5.0 %copy-start.10 = (f32[2048]{0:T(1024)S(1)}, f32[2048]{0:T(1024)}, u32[]{:S(2)}) copy-start(f32[2048]{0:T(1024)} %param.20) | copy-start | bytes 24580
  343.8 107.7 %reduce-scatter.5.cloned.1.call-start = ((), (), s32[]{:S(2)}) async-start(), calls=%async_computation.6 | async-start | bytes 1966080 | tf_op jit(solution)/shard_map/reduce_scatter | solution.py:160
  417.3 6.1 %copy-start.8 = (bf16[64,2048]{1,0:T(8,128)(2,1)}, bf16[64,2048]{1,0:T(8,128)(2,1)S(1)}, u32[]{:S(2)}) copy-start(bf16[64,2048]{1,0:T(8,128)(2,1)S(1)} %add_convert_fusion) | copy-start | bytes 786436
  417.4 34.2 %copy-start.11 = (s32[96]{0:T(128)S(1)}, s32[96]{0:T(128)}, u32[]{:S(2)}) copy-start(s32[96]{0:T(128)} %get-tuple-element.184) | copy-start | bytes 1156
  453.8 1.0 copy-start.2
Sparse Core Ops, SparseCore 0:
  17.9 22.3 all-gather.3
  42.5 124.4 all-gather.5
  169.1 122.6 all-gather.7
  344.0 72.0 reduce-scatter.2
  423.5 27.9 reduce-scatter.4
where the time goes:
time: 463 us; the launch traced here: 461 us
  waiting for transfers between devices  324 us (70%)
  local copies, waits for them, and re-layouts  66.4 us (14%)
  other arithmetic  32.7 us (7%)
  between operations  16 us (3%)
  matrix products  11.1 us (2%)
  loops' own time  10.5 us (2%)
    all_gather x1, waiting for transfers between devices, local(): key_piece = lax.all_gather(first_keys, 'ctx', axis=0, tiled=True)  107 us
    all_gather x1, waiting for transfers between devices, local(): value_piece = lax.all_gather(first_values, 'ctx', axis=0, tiled=True)  103 us
    reduce_scatter x1, waiting for transfers between devices, local(): lax.psum_scatter(jnp.dot(attended, w_out, preferred_element_type=jnp.floa...  68 us
    reduce_scatter x1, waiting for transfers between devices, local(): lax.psum_scatter(returning.astype(jnp.bfloat16), 'pack', scatter_dimensio...  28.1 us
    while x3, local copies, waits for them, and re-layouts, local(): lax.scan(visit, running, (jnp.arange(blocks, dtype=jnp.int32), key_stack,...  19.4 us
    all_gather x1, waiting for transfers between devices, local(): gathered = lax.all_gather(outgoing, 'pack', axis=0, tiled=True)  16.7 us
    reshape x1, local copies, waits for them, and re-layouts, local(): key_stack = key_piece.reshape(blocks, span_len, head_count, HD)  12.7 us
    reshape x1, local copies, waits for them, and re-layouts, local(): value_stack = value_piece.reshape(blocks, span_len, head_count, HD)  12.5 us
  transfers between devices with their start and end apart: 5, of which 5 were waited for; matrix products, arithmetic and copies ran while one was open for 11% of the time, Pallas kernels for 0%

commit v1 on v0

--- a/solution.py
+++ b/solution.py
@@ -7,6 +7,19 @@
 HD = 128
 epsilon = 1e-06
 very_negative = -1e30
+
+
+def ring_gather(array, axis, dim):
+    ways = lax.axis_size(axis)
+    up = [(d, (d + 1) % ways) for d in range(ways)]
+    down = [(d, (d - 1) % ways) for d in range(ways)]
+    earlier, later = ([array], [array])
+    for _ in range(ways // 2):
+        earlier.append(lax.ppermute(earlier[-1], axis, up))
+    for _ in range((ways - 1) // 2):
+        later.append(lax.ppermute(later[-1], axis, down))
+    line = jnp.concatenate([*earlier[::-1], *later[1:]], axis=dim)
+    return jnp.roll(line, (lax.axis_index(axis) - ways // 2) * array.shape[dim], axis=dim)
 
 
 def rotate(projected, position, head_count):
@@ -116,7 +129,7 @@
     )
     wanted = pattern[span_id]
     running = own_state
-    key_piece = lax.all_gather(first_keys, "ctx", axis=0, tiled=True)
+    key_piece = ring_gather(first_keys, "ctx", 0)
     value_piece = lax.all_gather(first_values, "ctx", axis=0, tiled=True)
     blocks = key_piece.shape[0] // span_len
     key_stack = key_piece.reshape(blocks, span_len, head_count, HD)

time: 463 us -> 473 us (1.022)
  waiting for transfers between devices: 324 us -> 276 us
  local copies, waits for them, and re-layouts: 66.4 us -> 105 us
  starting transfers between devices: 0.2 us -> 19 us
    ppermute x0 -> x7, waiting for transfers between devices: none -> 175 us  [the longest x4 174 us: ring_gather(): earlier.append(lax.ppermute(earlier[-1], axis, up))]
    all_gather x1 -> x0, waiting for transfers between devices: 107 us -> none  [local(): key_piece = lax.all_gather(first_keys, 'ctx', axis=0, tiled=True)]
    all_gather x1, waiting for transfers between devices: 103 us -> 0.01 us  [local(): value_piece = lax.all_gather(first_values, 'ctx', axis=0, tiled=True)]
    unnamed x23 -> x40, local copies, waits for them, and re-layouts: 2.38 us -> 31.9 us
    ppermute x0 -> x7, starting transfers between devices: none -> 18.7 us  [the longest x4 10.5 us: ring_gather(): earlier.append(lax.ppermute(earlier[-1], axis, up))]
    all_gather x1, waiting for transfers between devices: 16.7 us -> 0.01 us  [local(): gathered = lax.all_gather(outgoing, 'pack', axis=0, tiled=True)]
    dynamic_slice x0 -> x1, local copies, waits for them, and re-layouts: none -> 7.14 us  [ring_gather(): jnp.roll(line, (lax.axis_index(axis) - ways // 2) * array.shape[dim], axi...]
  transfers between devices with their start and end apart: 5 -> 11, of which waited for: 5 -> 7; matrix products, arithmetic and copies ran while one was open for 11% -> 19% of each run, Pallas kernels for 0% -> 0%
where the time goes in v1:
time: 473 us; the launch traced here: 470 us
  waiting for transfers between devices  276 us (58%)
  local copies, waits for them, and re-layouts  105 us (22%)
  other arithmetic  33.7 us (7%)
  starting transfers between devices  19 us (4%)
  between operations  16 us (3%)
  matrix products  11 us (2%)
  loops' own time  9.89 us (2%)
    ppermute x4, waiting for transfers between devices, ring_gather(): earlier.append(lax.ppermute(earlier[-1], axis, up))  174 us
    reduce_scatter x1, waiting for transfers between devices, local(): lax.psum_scatter(jnp.dot(attended, w_out, preferred_element_type=jnp.floa...  71.4 us
    unnamed x40, local copies, waits for them, and re-layouts  31.9 us
    reduce_scatter x1, waiting for transfers between devices, local(): lax.psum_scatter(returning.astype(jnp.bfloat16), 'pack', scatter_dimensio...  28.2 us
    while x3, local copies, waits for them, and re-layouts, local(): lax.scan(visit, running, (jnp.arange(blocks, dtype=jnp.int32), key_stack,...  19.4 us
    reshape x1, local copies, waits for them, and re-layouts, local(): value_stack = value_piece.reshape(blocks, span_len, head_count, HD)  12.5 us
    reshape x1, local copies, waits for them, and re-layouts, local(): key_stack = key_piece.reshape(blocks, span_len, head_count, HD)  12.5 us
    ppermute x4, starting transfers between devices, ring_gather(): earlier.append(lax.ppermute(earlier[-1], axis, up))  10.5 us
  transfers between devices with their start and end apart: 11, of which 7 were waited for; matrix products, arithmetic and copies ran while one was open for 19% of the time, Pallas kernels for 0%

profile of v1, /device:TPU:0, one launch (start us, length us, event | category | flops | bytes accessed | tf_op | source)
XLA Modules:
  0.0 470.2 jit_solution(17724178534697085532)
XLA Ops:
  19.2 3.0 collective-permute-start
  22.2 3.1 collective-permute-start.4
  27.3 51.3 %collective-permute-done = bf16[1024,512]{1,0:T(8,128)(2,1)} collective-permute-done((bf16[1024,512]{1,0:T(8,128)(2,1)}, bf16[1024,512]{1,0:T(8,128)(2,1)}, u32[]{:S(2)}, u32[]{:S(2)}) %collective-permute-start) | collective-permute-done | bytes 1048608 | tf_op jit(solution)/shard_map/ppermute | solution.py:18
  78.7 2.5 collective-permute-start.1
  81.2 3.0 collective-permute-start.5
  87.1 46.2 %collective-permute-done.1 = bf16[1024,512]{1,0:T(8,128)(2,1)} collective-permute-done((bf16[1024,512]{1,0:T(8,128)(2,1)}, bf16[1024,512]{1,0:T(8,128)(2,1)}, u32[]{:S(2)}, u32[]{:S(2)}) %collective-permute-start.1) | collective-permute-done | bytes 1048608 | tf_op jit(solution)/shard_map/ppermute | solution.py:18
  133.4 2.5 collective-permute-start.2
  138.9 4.9 %gather_fusion.2 = bf16[256,2048]{1,0:T(8,128)(2,1)} fusion(bf16[384,2048]{1,0:T(8,128)(2,1)} %all-gather.3.cloned.1.call-done, s32[1024]{0:T(1024)S(1)} %pad_clamp_fusion), kind=kCustom, calls=%fused_computation.2 | custom fusion | bytes 2098176 | tf_op jit(solution)/shard_map/gather | solution.py:115
  145.4 3.5 fusion.41
  152.9 50.2 %collective-permute-done.2 = bf16[1024,512]{1,0:T(8,128)(2,1)} collective-permute-done((bf16[1024,512]{1,0:T(8,128)(2,1)}, bf16[1024,512]{1,0:T(8,128)(2,1)}, u32[]{:S(2)}, u32[]{:S(2)}) %collective-permute-start.2) | collective-permute-done | bytes 1048608 | tf_op jit(solution)/shard_map/ppermute | solution.py:18
  203.1 2.5 collective-permute-start.3
  211.3 26.6 %collective-permute-done.3 = bf16[1024,512]{1,0:T(8,128)(2,1)S(1)} collective-permute-done((bf16[1024,512]{1,0:T(8,128)(2,1)}, bf16[1024,512]{1,0:T(8,128)(2,1)S(1)}, u32[]{:S(2)}, u32[]{:S(2)}) %collective-permute-start.3) | collective-permute-done | bytes 1048608 | tf_op jit(solution)/shard_map/ppermute | solution.py:18
  238.9 2.3 constant_dynamic-update-slice_fusion.14
  241.2 2.4 constant_dynamic-update-slice_fusion.13
  243.6 2.3 constant_dynamic-update-slice_fusion.12
  246.9 2.3 constant_dynamic-update-slice_fusion.10
  249.2 2.3 constant_dynamic-update-slice_fusion.9
  251.5 2.3 constant_dynamic-update-slice_fusion.8
  259.4 2.3 constant_dynamic-update-slice_fusion.4
  262.8 2.3 constant_dynamic-update-slice_fusion.2
  265.1 2.3 constant_dynamic-update-slice_fusion.1
  269.6 7.1 %constant_dynamic-slice_fusion = bf16[8192,512]{1,0:T(8,128)(2,1)} fusion(bf16[16384,512]{1,0:T(8,128)(2,1)} %constant_dynamic-update-slice_fusion, s32[]{:T(128)S(6)} %select_n.113), kind=kLoop, calls=%fused_computation.110 | loop fusion | bytes 16777220 | tf_op jit(solution)/shard_map/jit(_roll_dynamic)/dynamic_slice | solution.py:22
  276.8 12.5 %reshape.295 = bf16[8,1024,4,128]{3,2,1,0:T(4,128)(2,1)} reshape(bf16[8192,512]{1,0:T(8,128)(2,1)} %constant_dynamic-slice_fusion) | data formatting | bytes 16777216 | tf_op jit(solution)/shard_map/reshape | solution.py:135
  289.3 8.7 %copy.34 = bf16[8,1024,4,128]{3,1,2,0:T(8,128)(2,1)} copy(bf16[8,1024,4,128]{3,2,1,0:T(4,128)(2,1)} %reshape.295) | data formatting | bytes 16777216 | tf_op jit(solution)/shard_map/while | solution.py:149
  298.0 12.5 %reshape.296 = bf16[8,1024,4,128]{3,2,1,0:T(4,128)(2,1)} reshape(bf16[8192,512]{1,0:T(8,128)(2,1)} %all-gather.5.cloned.1.call-done) | data formatting | bytes 16777216 | tf_op jit(solution)/shard_map/reshape | solution.py:136
  310.6 8.7 %copy.35 = bf16[8,1024,4,128]{3,1,2,0:T(8,128)(2,1)} copy(bf16[8,1024,4,128]{3,2,1,0:T(4,128)(2,1)} %reshape.296) | data formatting | bytes 16777216 | tf_op jit(solution)/shard_map/while | solution.py:149
  319.2 24.6 %while.14 = (s32[]{:T(128)}, f32[4,256]{1,0:T(4,128)S(1)}, f32[4,256]{1,0:T(4,128)S(1)}, f32[256,4,128]{2,0,1:T(8,128)}, s32[8]{0:T(128)S(1)}, /*index=5*/s32[]{...) while((s32[]{:T(128)}, f32[4,256]{1,0:T(4,128)S(1)}, ...), condition=%wide.region_13.14_spmd, body=%wide.region_7.13_spmd.sunk | while | flops 545657856 | bytes 20264296 | solution.py:149
  349.4 2.8 convert_element_type.45
  353.5 71.4 %reduce-scatter.3.cloned.1.call-done = f32[64,2048]{1,0:T(8,128)} async-done(((f32[256,2048]{1,0:T(8,128)}), f32[64,2048]{1,0:T(8,128)}) %reduce-scatter.3.cloned.1.call-update) | async-done | bytes 524304 | tf_op jit(solution)/shard_map/reduce_scatter | solution.py:157
  426.2 2.7 scatter_custom_fusion
  428.9 3.3 convert_element_type.53
  432.2 28.2 %reduce-scatter.5.cloned.1.call-done = bf16[96,2048]{1,0:T(8,128)(2,1)} async-done(((bf16[384,2048]{1,0:T(8,128)(2,1)}), bf16[96,2048]{1,0:T(8,128)(2,1)}) %reduce-scatter.5.cloned.1.call-update) | async-done | bytes 393232 | tf_op jit(solution)/shard_map/reduce_scatter | solution.py:173
  (108 shorter events, 66.3 us)
Async XLA Ops:
  7.2 339.8 %copy-start = (bf16[512,2048]{1,0:T(8,128)(2,1)S(1)}, bf16[512,2048]{1,0:T(8,128)(2,1)}, u32[]{:S(2)}) copy-start(bf16[512,2048]{1,0:T(8,128)(2,1)} %param.18) | copy-start | bytes 6291460
  7.2 18.2 %copy-start.1 = (s32[1,256]{1,0:T(1,128)S(1)}, s32[1,256]{1,0:T(1,128)}, u32[]{:S(2)}) copy-start(s32[1,256]{1,0:T(1,128)} %param.21) | copy-start | bytes 3076
  7.2 78.5 %copy-start.9 = (s32[1,256]{1,0:T(1,128)S(1)}, s32[1,256]{1,0:T(1,128)}, u32[]{:S(2)}) copy-start(s32[1,256]{1,0:T(1,128)} %param.22) | copy-start | bytes 3076
  7.2 131.7 %all-gather.3.cloned.1.call-start = ((), (), s32[]{:S(2)}) async-start(), calls=%async_computation.2 | async-start | bytes 1966080 | tf_op jit(solution)/shard_map/all_gather | solution.py:108
  9.5 6.6 %copy-start.11 = (s32[4]{0:T(128)}, s32[4]{0:T(128)S(1)}, u32[]{:S(2)}) copy-start(s32[4]{0:T(128)S(1)} %convert_reduce_fusion) | copy-start | bytes 52
  18.4 279.6 %all-gather.5.cloned.1.call-start = ((), (), s32[]{:S(2)}) async-start(), calls=%async_computation.3 | async-start | bytes 9437184 | tf_op jit(solution)/shard_map/all_gather | solution.py:133
  19.1 405.7 %reduce-scatter.3.cloned.1.call-start = ((), (), s32[]{:S(2)}) async-start(), calls=%async_computation.4 | async-start | bytes 2621440 | tf_op jit(solution)/shard_map/reduce_scatter | solution.py:157
  19.2 59.5 %collective-permute-start = (bf16[1024,512]{1,0:T(8,128)(2,1)}, bf16[1024,512]{1,0:T(8,128)(2,1)}, u32[]{:S(2)}, u32[]{:S(2)}) collective-permute-start(bf16[1024,512]{1,0:T(8,128)(2,1)} %param.15), channel_id=1, source_target_pairs={{0,4},{4,8},{8,12},{12,16},{16,20},{20,24},{24,28},{28,0},{1,5},{5... | collective-permute-start | bytes 3145736 | tf_op jit(solution)/shard_map/ppermute | solution.py:18
  22.2 58.9 %collective-permute-start.4 = (bf16[1024,512]{1,0:T(8,128)(2,1)}, bf16[1024,512]{1,0:T(8,128)(2,1)}, u32[]{:S(2)}, u32[]{:S(2)}) collective-permute-start(bf16[1024,512]{1,0:T(8,128)(2,1)} %param.15), channel_id=1, source_target_pairs={{0,28},{4,0},{8,4},{12,8},{16,12},{20,16},{24,20},{28,24},{1,29},{... | collective-permute-start | bytes 3145736 | tf_op jit(solution)/shard_map/ppermute | solution.py:20
  78.7 54.7 %collective-permute-start.1 = (bf16[1024,512]{1,0:T(8,128)(2,1)}, bf16[1024,512]{1,0:T(8,128)(2,1)}, u32[]{:S(2)}, u32[]{:S(2)}) collective-permute-start(bf16[1024,512]{1,0:T(8,128)(2,1)} %collective-permute-done), channel_id=1, source_target_pairs={{0,4},{4,8},{8,12},{12,16},{16,20},{20,24},{24,28},{28,0},{1,5},{5... | collective-permute-start | bytes 3145736 | tf_op jit(solution)/shard_map/ppermute | solution.py:18
  81.2 55.8 %collective-permute-start.5 = (bf16[1024,512]{1,0:T(8,128)(2,1)}, bf16[1024,512]{1,0:T(8,128)(2,1)}, u32[]{:S(2)}, u32[]{:S(2)}) collective-permute-start(bf16[1024,512]{1,0:T(8,128)(2,1)} %collective-permute-done.4), channel_id=1, source_target_pairs={{0,28},{4,0},{8,4},{12,8},{16,12},{20,16},{24,20},{28,24},{1,29},{... | collective-permute-start | bytes 3145736 | tf_op jit(solution)/shard_map/ppermute | solution.py:20
  87.1 58.3 %copy-start.13 = (f32[2048]{0:T(1024)S(1)}, f32[2048]{0:T(1024)}, u32[]{:S(2)}) copy-start(f32[2048]{0:T(1024)} %param.19) | copy-start | bytes 24580
  133.4 69.7 %collective-permute-start.2 = (bf16[1024,512]{1,0:T(8,128)(2,1)}, bf16[1024,512]{1,0:T(8,128)(2,1)}, u32[]{:S(2)}, u32[]{:S(2)}) collective-permute-start(bf16[1024,512]{1,0:T(8,128)(2,1)} %collective-permute-done.1), channel_id=1, source_target_pairs={{0,4},{4,8},{8,12},{12,16},{16,20},{20,24},{24,28},{28,0},{1,5},{5... | collective-permute-start | bytes 3145736 | tf_op jit(solution)/shard_map/ppermute | solution.py:18
  136.9 114.6 %collective-permute-start.6 = (bf16[1024,512]{1,0:T(8,128)(2,1)}, bf16[1024,512]{1,0:T(8,128)(2,1)}, u32[]{:S(2)}, u32[]{:S(2)}) collective-permute-start(bf16[1024,512]{1,0:T(8,128)(2,1)} %collective-permute-done.5), channel_id=1, source_target_pairs={{0,28},{4,0},{8,4},{12,8},{16,12},{20,16},{24,20},{28,24},{1,29},{... | collective-permute-start | bytes 3145736 | tf_op jit(solution)/shard_map/ppermute | solution.py:20
  150.9 54.6 %copy-start.5 = (bf16[1024,512]{1,0:T(8,128)(2,1)S(1)}, bf16[1024,512]{1,0:T(8,128)(2,1)}, u32[]{:S(2)}) copy-start(bf16[1024,512]{1,0:T(8,128)(2,1)} %param.15) | copy-start | bytes 3145732
  152.5 55.0 %copy-start.6 = (pred[256,1024]{1,0:T(8,128)(4,1)S(1)}, pred[256,1024]{1,0:T(8,128)(4,1)}, u32[]{:S(2)}) copy-start(pred[256,1024]{1,0:T(8,128)(4,1)} %broadcast_compare_fusion) | copy-start | bytes 786436
  152.5 55.0 %copy-start.7 = (bf16[1024,512]{1,0:T(8,128)(2,1)S(1)}, bf16[1024,512]{1,0:T(8,128)(2,1)}, u32[]{:S(2)}) copy-start(bf16[1024,512]{1,0:T(8,128)(2,1)} %param.16) | copy-start | bytes 3145732
  203.1 34.8 %collective-permute-start.3 = (bf16[1024,512]{1,0:T(8,128)(2,1)}, bf16[1024,512]{1,0:T(8,128)(2,1)S(1)}, u32[]{:S(2)}, u32[]{:S(2)}) collective-permute-start(bf16[1024,512]{1,0:T(8,128)(2,1)} %collective-permute-done.2), channel_id=1, source_target_pairs={{0,4},{4,8},{8,12},{12,16},{16,20},{20,24},{24,28},{28,0},{1,5},{5... | collective-permute-start | bytes 3145736 | tf_op jit(solution)/shard_map/ppermute | solution.py:18
  347.0 5.3 %copy-start.10 = (f32[2048]{0:T(1024)S(1)}, f32[2048]{0:T(1024)}, u32[]{:S(2)}) copy-start(f32[2048]{0:T(1024)} %param.20) | copy-start | bytes 24580
  349.1 111.4 %reduce-scatter.5.cloned.1.call-start = ((), (), s32[]{:S(2)}) async-start(), calls=%async_computation.5 | async-start | bytes 1966080 | tf_op jit(solution)/shard_map/reduce_scatter | solution.py:173
  426.1 6.1 %copy-start.8 = (bf16[64,2048]{1,0:T(8,128)(2,1)}, bf16[64,2048]{1,0:T(8,128)(2,1)S(1)}, u32[]{:S(2)}) copy-start(bf16[64,2048]{1,0:T(8,128)(2,1)S(1)} %add_convert_fusion) | copy-start | bytes 786436
  426.2 34.3 %copy-start.12 = (s32[96]{0:T(128)S(1)}, s32[96]{0:T(128)}, u32[]{:S(2)}) copy-start(s32[96]{0:T(128)} %get-tuple-element.184) | copy-start | bytes 1156
  462.6 1.0 copy-start.2
Sparse Core Ops, SparseCore 0:
  18.5 22.3 all-gather.2
  43.0 224.1 all-gather.4
  349.2 75.6 reduce-scatter.2
  432.3 28.0 reduce-scatter.4
